TPU v7x, 256 devices: a whole 4x4x8 slice. The times are simulated.
256 devices in a mesh: dp: 4 (over y), segment: 8 (over z_hi, x), chan: 8 (over z_lo, core).
Axes of the slice: x: 4, y: 4, z: 8 (z_hi: 2, z_lo: 4; z = z_hi * 4 + z_lo), core: 2. Of those that a mesh axis runs over, the one named last changes fastest.
Arguments:
- x_input: bfloat16 [4, 4, 256, 1024], P(None, 'dp', None, 'chan'), may hold values from -48 to 48
- d_output: bfloat16 [4, 4, 256, 1024], P(None, 'dp', None, 'chan'), may hold values from -6 to 6
- weights: bfloat16 [8, 9, 1024, 1024], P('segment', None, None, 'chan'), may hold values from -0.0625 to 0.0625
- gains: float32 [8, 1024], P('segment', 'chan'), may hold values from 0.5 to 1.5
- biases: float32 [8, 1024], P('segment', 'chan'), may hold values from -3 to 3
Outputs:
- d_weights: float32 [8, 9, 1024, 1024], P('segment', None, None, 'chan')
- d_gains: float32 [8, 1024], P('segment', 'chan')
- d_biases: float32 [8, 1024], P('segment', 'chan')
All inputs are finite; a program needn't handle non-finite values.
Results may differ from a plain program's by a relative error of at most 0.025.
Values may be sent and summed in bfloat16 or wider, within the bound.
No kernel may reach another device: no remote copies, remote signals or barrier semaphores. Data moves between devices by JAX's collectives and lax.ppermute only.
A program may use at most 64 MiB of HBM per device.

v0:
```python
import jax
import jax.numpy as jnp
from jax import lax
from jax.sharding import PartitionSpec as P

GROUPS = 32
SIDE = 16
EPSILON = 1e-05


def shifted(shard, axis, by):
    length = lax.axis_size(axis)
    pairs = [(i, i + by) for i in range(length) if 0 <= i + by < length]
    return lax.ppermute(shard, axis, pairs)


def expand_groups(statistic, group_width):
    return jnp.repeat(statistic, group_width, axis=1)[:, None, :]


def group_sums(values, group_width):
    batch_count, pixel_count, channels = values.shape
    grouped = values.reshape(batch_count, pixel_count, channels // group_width, group_width)
    return jnp.sum(grouped, axis=(1, 3))


def shifted_stack(images, forward_taps):
    batch_count, pixel_count, channels = images.shape
    square = images.reshape(batch_count, SIDE, SIDE, channels)
    padded = jnp.pad(square, ((0, 0), (1, 1), (1, 1), (0, 0)))
    tap_list = []
    for tap_y in range(3):
        for tap_x in range(3):
            start_y = tap_y if forward_taps else 2 - tap_y
            start_x = tap_x if forward_taps else 2 - tap_x
            window = padded[:, start_y : start_y + SIDE, start_x : start_x + SIDE, :]
            tap_list.append(window.reshape(batch_count * pixel_count, channels))
    return jnp.stack(tap_list)


def take_slot(buffer, slot_index):
    return lax.dynamic_index_in_dim(buffer, slot_index, 0, keepdims=False)


def put_slot(buffer, value, slot_index, allowed):
    current = take_slot(buffer, slot_index)
    return lax.dynamic_update_index_in_dim(
        buffer, jnp.where(allowed, value, current), slot_index, 0
    )


def local(x_input, d_output, weights, gains, biases):
    segments = lax.axis_size("segment")
    half_way = segments // 2
    position = lax.axis_index("segment")
    is_down = position < half_way
    level = jnp.where(is_down, position, 2 * half_way - 1 - position)
    weight = weights[0]
    gain_row = gains[0]
    bias_row = biases[0]
    micro_count, images, pixels, local_width = x_input.shape
    full_width = weight.shape[1]
    group_width = full_width // GROUPS
    local_groups = local_width // group_width
    row_count = images * pixels
    group_count = pixels * group_width
    tick_count = micro_count + segments - 1
    bwd_place = 2 * half_way - 1 - position
    act_shape = (images, pixels, local_width)
    below_slot = jnp.clip(position - 1, 0, half_way - 1)
    above_slot = jnp.clip(level + 1, 0, half_way - 1)
    has_above = level < half_way - 1
    before_slot = jnp.clip(level - 1, 0, half_way - 1)

    def normalize(values, group_mean, group_rstd):
        normed = (values - expand_groups(group_mean, group_width)) * expand_groups(
            group_rstd, group_width
        )
        return (normed, normed * gain_row + bias_row)

    def forward_tick(tick_index, loop_state):
        stack_recv, saved_inputs, saved_mean, saved_rstd, saved_full = loop_state
        micro_index = tick_index - position
        active = (micro_index >= 0) & (micro_index < micro_count)
        slot_index = jnp.clip(micro_index, 0, micro_count - 1)
        first_in = jnp.where(
            position == 0, take_slot(x_input, slot_index), take_slot(stack_recv, below_slot)
        )
        skip_part = take_slot(stack_recv, level).astype(jnp.float32)
        upper_part = jnp.where(
            has_above, take_slot(stack_recv, above_slot).astype(jnp.float32), 0.0
        )
        joined = (upper_part + skip_part).astype(jnp.bfloat16)
        inputs = jnp.where(is_down, first_in, joined)
        values = inputs.astype(jnp.float32)
        group_mean = group_sums(values, group_width) / group_count
        centred = values - expand_groups(group_mean, group_width)
        variance = group_sums(centred * centred, group_width) / group_count
        group_rstd = lax.rsqrt(variance + EPSILON)
        normed, pre_act = normalize(values, group_mean, group_rstd)
        hidden = (pre_act * jax.nn.sigmoid(pre_act)).astype(jnp.bfloat16)
        empty_sum = jnp.zeros((row_count, local_width), jnp.float32)
        shard_piece = lax.all_gather(hidden, "chan", axis=2, tiled=True)
        conv_out = lax.cond(
            active,
            lambda: empty_sum
            + jnp.einsum(
                "trc,tco->ro",
                shifted_stack(shard_piece, True),
                weight,
                preferred_element_type=jnp.float32,
            ),
            lambda: empty_sum,
        )
        output = (values + conv_out.reshape(act_shape)).astype(jnp.bfloat16)
        saved_inputs = put_slot(saved_inputs, inputs, slot_index, active)
        saved_mean = put_slot(saved_mean, group_mean, slot_index, active)
        saved_rstd = put_slot(saved_rstd, group_rstd, slot_index, active)
        outgoing = put_slot(stack_recv, output, level, True)
        next_stack = shifted(outgoing, "segment", 1)
        return (next_stack, saved_inputs, saved_mean, saved_rstd, saved_full)

    zero_stack = jnp.zeros((half_way,) + act_shape, jnp.bfloat16)
    zero_buffer = jnp.zeros((micro_count,) + act_shape, jnp.bfloat16)
    zero_stats = jnp.zeros((micro_count, images, local_groups), jnp.float32)
    full_init = jnp.zeros((1,), jnp.bfloat16)
    forward_state = lax.fori_loop(
        0, tick_count, forward_tick, (zero_stack, zero_buffer, zero_stats, zero_stats, full_init)
    )
    saved_inputs, saved_mean, saved_rstd, saved_full = (
        forward_state[1],
        forward_state[2],
        forward_state[3],
        forward_state[4],
    )

    def backward_tick(tick_index, loop_state):
        grad_stack, grad_weight, grad_gain, grad_bias = loop_state
        micro_index = tick_index - bwd_place
        active = (micro_index >= 0) & (micro_index < micro_count)
        slot_index = jnp.clip(micro_index, 0, micro_count - 1)
        own_part = take_slot(grad_stack, level).astype(jnp.float32)
        later_part = jnp.where(
            has_above, take_slot(grad_stack, above_slot).astype(jnp.float32), 0.0
        )
        down_grad = (own_part + later_part).astype(jnp.bfloat16)
        up_grad = jnp.where(
            level == 0, take_slot(d_output, slot_index), take_slot(grad_stack, before_slot)
        )
        grad_out = jnp.where(is_down, down_grad, up_grad)
        values = take_slot(saved_inputs, slot_index).astype(jnp.float32)
        group_mean = take_slot(saved_mean, slot_index)
        group_rstd = take_slot(saved_rstd, slot_index)
        normed, pre_act = normalize(values, group_mean, group_rstd)
        sigma = jax.nn.sigmoid(pre_act)
        grad_rows = grad_out.reshape(row_count, local_width)
        hidden = (pre_act * sigma).astype(jnp.bfloat16)
        shard_piece = lax.all_gather(hidden, "chan", axis=2, tiled=True)
        grad_weight = grad_weight + lax.cond(
            active,
            lambda: jnp.einsum(
                "trc,ro->tco",
                shifted_stack(shard_piece, True),
                grad_rows,
                preferred_element_type=jnp.float32,
            ),
            lambda: jnp.zeros((9, shard_piece.shape[2], local_width), jnp.float32),
        )
        partial_grad = lax.cond(
            active,
            lambda: jnp.einsum(
                "tro,tco->rc",
                shifted_stack(grad_out, False),
                weight,
                preferred_element_type=jnp.float32,
            ),
            lambda: jnp.zeros((row_count, full_width), jnp.float32),
        )
        grad_hidden = lax.psum_scatter(
            partial_grad.reshape(images, pixels, full_width).astype(jnp.bfloat16),
            "chan",
            scatter_dimension=2,
            tiled=True,
        ).astype(jnp.float32)
        grad_pre = grad_hidden * sigma * (1.0 + pre_act * (1.0 - sigma))
        grad_gain = grad_gain + jnp.where(active, jnp.sum(grad_pre * normed, axis=(0, 1)), 0.0)
        grad_bias = grad_bias + jnp.where(active, jnp.sum(grad_pre, axis=(0, 1)), 0.0)
        grad_normed = grad_pre * gain_row
        first_mean = expand_groups(group_sums(grad_normed, group_width) / group_count, group_width)
        second_mean = expand_groups(
            group_sums(grad_normed * normed, group_width) / group_count, group_width
        )
        grad_in = (
            grad_out.astype(jnp.float32)
            + expand_groups(group_rstd, group_width)
            * (grad_normed - first_mean - normed * second_mean)
        ).astype(jnp.bfloat16)
        outgoing = put_slot(grad_stack, grad_in, level, True)
        next_stack = shifted(outgoing, "segment", -1)
        return (next_stack, grad_weight, grad_gain, grad_bias)

    backward_init = (
        zero_stack,
        jnp.zeros(weight.shape, jnp.float32),
        jnp.zeros((local_width,), jnp.float32),
        jnp.zeros((local_width,), jnp.float32),
    )
    backward_state = lax.fori_loop(0, tick_count, backward_tick, backward_init)
    grad_weight, grad_gain, grad_bias = (
        lax.psum(backward_state[1].astype(jnp.bfloat16), "dp").astype(jnp.float32),
        lax.psum(backward_state[2].astype(jnp.bfloat16), "dp").astype(jnp.float32),
        lax.psum(backward_state[3].astype(jnp.bfloat16), "dp").astype(jnp.float32),
    )
    return (grad_weight[None], grad_gain[None], grad_bias[None])


def solution(mesh):
    in_specs = (
        P(None, "dp", None, "chan"),
        P(None, "dp", None, "chan"),
        P("segment", None, None, "chan"),
        P("segment", "chan"),
        P("segment", "chan"),
    )
    out_specs = (P("segment", None, None, "chan"), P("segment", "chan"), P("segment", "chan"))
    return jax.shard_map(local, mesh=mesh, in_specs=in_specs, out_specs=out_specs, check_vma=False)
```

profile of v0, /device:TPU:1, one launch (start us, length us, event | category | flops | bytes accessed | tf_op | source)
XLA Modules:
  0.0 1573.2 jit_solution(6133271358537587081)
XLA Ops:
  8.2 388.7 %while.47 = (s32[]{:T(128)}, bf16[4,1,256,128]{3,2,1,0:T(8,128)(2,1)S(1)}, bf16[4,1,256,128]{3,2,1,0:T(8,128)(2,1)S(1)}, f32[4,1,4]{2,1,0:T(1,128)S(1)}, f32[4,1...) while((s32[]{:T(128)}, ...), condition=%wide.region_7.8_spmd, body=%wide.region_0.7_spmd.sunk | while | flops 604864512 | bytes 33960956 | solution.py:127
  10.7 16.7 %all_gather.25 = bf16[1,256,1024]{2,1,0:T(8,128)(2,1)S(1)} all-gather(bf16[1,256,128]{2,1,0:T(8,128)(2,1)S(1)} %fusion.67), channel_id=1, replica_groups=mesh['dp'=4,'segment'=8,'chan'=8] {'chan'}, dimensions={2}, use_global_device_ids=true | all-gather | bytes 589824 | tf_op jit(solution)/shard_map/while/body/eval_jaxpr/all_gather | solution.py:103
  40.8 14.4 all_gather.25
  71.2 14.9 all_gather.25
  102.1 14.9 all_gather.25
  132.9 14.9 all_gather.25
  147.8 13.5 collective-permute-start
  169.4 14.9 all_gather.25
  184.3 14.2 collective-permute-start
  206.6 14.9 all_gather.25
  221.5 14.1 collective-permute-start
  243.7 14.9 all_gather.25
  258.6 14.1 collective-permute-start
  280.7 14.9 all_gather.25
  295.7 17.8 %collective-permute-start = (bf16[4,1,256,128]{3,2,1,0:T(8,128)(2,1)S(1)}, bf16[4,1,256,128]{3,2,1,0:T(8,128)(2,1)S(1)}, u32[]{:S(2)}, u32[]{:S(2)}) collective-permute-start(bf16[4,1,256,128]{3,2,1,0:T(8,128)(2,1)S(1)} %fusion.68), channel_id=1, source_target_pairs={{0,8},{8,16},{16,24},{24,32},{32,40},{40,48},{48,56},{1,9},{9,17},... | collective-permute-start | bytes 786440 | tf_op jit(solution)/shard_map/while/body/eval_jaxpr/ppermute | solution.py:14
  321.5 14.9 all_gather.25
  336.5 14.1 collective-permute-start
  358.6 14.9 all_gather.25
  373.6 17.8 %collective-permute-start = (bf16[4,1,256,128]{3,2,1,0:T(8,128)(2,1)S(1)}, bf16[4,1,256,128]{3,2,1,0:T(8,128)(2,1)S(1)}, u32[]{:S(2)}, u32[]{:S(2)}) collective-permute-start(bf16[4,1,256,128]{3,2,1,0:T(8,128)(2,1)S(1)} %fusion.68), channel_id=1, source_target_pairs={{0,8},{8,16},{16,24},{24,32},{32,40},{40,48},{48,56},{1,9},{9,17},... | collective-permute-start | bytes 786440 | tf_op jit(solution)/shard_map/while/body/eval_jaxpr/ppermute | solution.py:14
  397.6 1098.8 %while.48 = (s32[]{:T(128)}, bf16[4,1,256,128]{3,2,1,0:T(8,128)(2,1)}, f32[9,1024,128]{2,1,0:T(8,128)}, f32[128]{0:T(128)S(1)}, f32[128]{0:T(128)S(1)}, /*index=...) while((s32[]{:T(128)}, ...), condition=%wide.region_20.21_spmd.clone, body=%wide.region_8.20_spmd.clone.sunk | while | flops 1211728384 | bytes 62218040 | solution.py:208
  400.9 69.3 %reduce-scatter.6.cloned.1.call-done = bf16[128,256]{1,0:T(8,128)(2,1)} async-done(((bf16[1024,256]{1,0:T(8,128)(2,1)}), bf16[128,256]{1,0:T(8,128)(2,1)}) %reduce-scatter.6.cloned.1.call-update) | async-done | bytes 65552 | tf_op jit(solution)/shard_map/while
  474.1 19.5 %all_gather.26 = bf16[1,256,1024]{2,1,0:T(8,128)(2,1)S(1)} all-gather(bf16[1,256,128]{2,1,0:T(8,128)(2,1)S(1)} %get-tuple-element.1489), channel_id=1, replica_groups=mesh['dp'=4,'segment'=8,'chan'=8] {'chan'}, dimensions={2}, use_global_device_ids=true | all-gather | bytes 589824 | tf_op jit(solution)/shard_map/while/body/eval_jaxpr/all_gather | solution.py:158
  506.2 58.9 %reduce-scatter.6.cloned.1.call-done = bf16[128,256]{1,0:T(8,128)(2,1)} async-done(((bf16[1024,256]{1,0:T(8,128)(2,1)}), bf16[128,256]{1,0:T(8,128)(2,1)}) %reduce-scatter.6.cloned.1.call-update) | async-done | bytes 65552 | tf_op jit(solution)/shard_map/while
  569.0 19.5 %all_gather.26 = bf16[1,256,1024]{2,1,0:T(8,128)(2,1)S(1)} all-gather(bf16[1,256,128]{2,1,0:T(8,128)(2,1)S(1)} %get-tuple-element.1489), channel_id=1, replica_groups=mesh['dp'=4,'segment'=8,'chan'=8] {'chan'}, dimensions={2}, use_global_device_ids=true | all-gather | bytes 589824 | tf_op jit(solution)/shard_map/while/body/eval_jaxpr/all_gather | solution.py:158
  602.5 58.7 %reduce-scatter.6.cloned.1.call-done = bf16[128,256]{1,0:T(8,128)(2,1)} async-done(((bf16[1024,256]{1,0:T(8,128)(2,1)}), bf16[128,256]{1,0:T(8,128)(2,1)}) %reduce-scatter.6.cloned.1.call-update) | async-done | bytes 65552 | tf_op jit(solution)/shard_map/while
  665.1 19.6 %all_gather.26 = bf16[1,256,1024]{2,1,0:T(8,128)(2,1)S(1)} all-gather(bf16[1,256,128]{2,1,0:T(8,128)(2,1)S(1)} %get-tuple-element.1489), channel_id=1, replica_groups=mesh['dp'=4,'segment'=8,'chan'=8] {'chan'}, dimensions={2}, use_global_device_ids=true | all-gather | bytes 589824 | tf_op jit(solution)/shard_map/while/body/eval_jaxpr/all_gather | solution.py:158
  698.7 58.8 %reduce-scatter.6.cloned.1.call-done = bf16[128,256]{1,0:T(8,128)(2,1)} async-done(((bf16[1024,256]{1,0:T(8,128)(2,1)}), bf16[128,256]{1,0:T(8,128)(2,1)}) %reduce-scatter.6.cloned.1.call-update) | async-done | bytes 65552 | tf_op jit(solution)/shard_map/while
  761.4 19.6 %all_gather.26 = bf16[1,256,1024]{2,1,0:T(8,128)(2,1)S(1)} all-gather(bf16[1,256,128]{2,1,0:T(8,128)(2,1)S(1)} %get-tuple-element.1489), channel_id=1, replica_groups=mesh['dp'=4,'segment'=8,'chan'=8] {'chan'}, dimensions={2}, use_global_device_ids=true | all-gather | bytes 589824 | tf_op jit(solution)/shard_map/while/body/eval_jaxpr/all_gather | solution.py:158
  795.1 63.4 %reduce-scatter.6.cloned.1.call-done = bf16[128,256]{1,0:T(8,128)(2,1)} async-done(((bf16[1024,256]{1,0:T(8,128)(2,1)}), bf16[128,256]{1,0:T(8,128)(2,1)}) %reduce-scatter.6.cloned.1.call-update) | async-done | bytes 65552 | tf_op jit(solution)/shard_map/while
  862.4 19.8 %all_gather.26 = bf16[1,256,1024]{2,1,0:T(8,128)(2,1)S(1)} all-gather(bf16[1,256,128]{2,1,0:T(8,128)(2,1)S(1)} %get-tuple-element.1489), channel_id=1, replica_groups=mesh['dp'=4,'segment'=8,'chan'=8] {'chan'}, dimensions={2}, use_global_device_ids=true | all-gather | bytes 589824 | tf_op jit(solution)/shard_map/while/body/eval_jaxpr/all_gather | solution.py:158
  896.1 63.4 %reduce-scatter.6.cloned.1.call-done = bf16[128,256]{1,0:T(8,128)(2,1)} async-done(((bf16[1024,256]{1,0:T(8,128)(2,1)}), bf16[128,256]{1,0:T(8,128)(2,1)}) %reduce-scatter.6.cloned.1.call-update) | async-done | bytes 65552 | tf_op jit(solution)/shard_map/while
  963.5 19.5 %all_gather.26 = bf16[1,256,1024]{2,1,0:T(8,128)(2,1)S(1)} all-gather(bf16[1,256,128]{2,1,0:T(8,128)(2,1)S(1)} %get-tuple-element.1489), channel_id=1, replica_groups=mesh['dp'=4,'segment'=8,'chan'=8] {'chan'}, dimensions={2}, use_global_device_ids=true | all-gather | bytes 589824 | tf_op jit(solution)/shard_map/while/body/eval_jaxpr/all_gather | solution.py:158
  997.0 63.4 %reduce-scatter.6.cloned.1.call-done = bf16[128,256]{1,0:T(8,128)(2,1)} async-done(((bf16[1024,256]{1,0:T(8,128)(2,1)}), bf16[128,256]{1,0:T(8,128)(2,1)}) %reduce-scatter.6.cloned.1.call-update) | async-done | bytes 65552 | tf_op jit(solution)/shard_map/while
  1064.3 19.6 %all_gather.26 = bf16[1,256,1024]{2,1,0:T(8,128)(2,1)S(1)} all-gather(bf16[1,256,128]{2,1,0:T(8,128)(2,1)S(1)} %get-tuple-element.1489), channel_id=1, replica_groups=mesh['dp'=4,'segment'=8,'chan'=8] {'chan'}, dimensions={2}, use_global_device_ids=true | all-gather | bytes 589824 | tf_op jit(solution)/shard_map/while/body/eval_jaxpr/all_gather | solution.py:158
  1100.7 58.3 %reduce-scatter.6.cloned.1.call-done = bf16[128,256]{1,0:T(8,128)(2,1)} async-done(((bf16[1024,256]{1,0:T(8,128)(2,1)}), bf16[128,256]{1,0:T(8,128)(2,1)}) %reduce-scatter.6.cloned.1.call-update) | async-done | bytes 65552 | tf_op jit(solution)/shard_map/while
  1162.9 19.5 %all_gather.26 = bf16[1,256,1024]{2,1,0:T(8,128)(2,1)S(1)} all-gather(bf16[1,256,128]{2,1,0:T(8,128)(2,1)S(1)} %get-tuple-element.1489), channel_id=1, replica_groups=mesh['dp'=4,'segment'=8,'chan'=8] {'chan'}, dimensions={2}, use_global_device_ids=true | all-gather | bytes 589824 | tf_op jit(solution)/shard_map/while/body/eval_jaxpr/all_gather | solution.py:158
  1182.4 27.5 %conditional.10 = (f32[9,1024,128]{2,1,0:T(8,128)}) conditional(s32[]{:T(128)} %convert_element_type.631, () %tuple.163, (bf16[1,256,1024]{2,1,0:T(8,128)(2,1)S(1)}, pred[]{:T(512)}, pred[]{:T(512)}, bf16[1,1,256,128]{3,2,1,0:T(8,128)(2,1)S(1)}, bf16[1,1,256,128]{3,2,1,0:T(8,128)(2,1)S(1)}, ...), branch_computations={%region_16.16_spmd, %region_17.17_spmd} | conditional | flops 604045312 | bytes 33226762 | solution.py:159
  1224.1 28.5 %reduce-scatter.6.cloned.1.call-done = bf16[128,256]{1,0:T(8,128)(2,1)} async-done(((bf16[1024,256]{1,0:T(8,128)(2,1)}), bf16[128,256]{1,0:T(8,128)(2,1)}) %reduce-scatter.6.cloned.1.call-update) | async-done | bytes 65552 | tf_op jit(solution)/shard_map/while
  1256.4 19.6 %all_gather.26 = bf16[1,256,1024]{2,1,0:T(8,128)(2,1)S(1)} all-gather(bf16[1,256,128]{2,1,0:T(8,128)(2,1)S(1)} %get-tuple-element.1489), channel_id=1, replica_groups=mesh['dp'=4,'segment'=8,'chan'=8] {'chan'}, dimensions={2}, use_global_device_ids=true | all-gather | bytes 589824 | tf_op jit(solution)/shard_map/while/body/eval_jaxpr/all_gather | solution.py:158
  1276.1 27.5 %conditional.10 = (f32[9,1024,128]{2,1,0:T(8,128)}) conditional(s32[]{:T(128)} %convert_element_type.631, () %tuple.163, (bf16[1,256,1024]{2,1,0:T(8,128)(2,1)S(1)}, pred[]{:T(512)}, pred[]{:T(512)}, bf16[1,1,256,128]{3,2,1,0:T(8,128)(2,1)S(1)}, bf16[1,1,256,128]{3,2,1,0:T(8,128)(2,1)S(1)}, ...), branch_computations={%region_16.16_spmd, %region_17.17_spmd} | conditional | flops 604045312 | bytes 33226762 | solution.py:159
  1317.8 27.1 %reduce-scatter.6.cloned.1.call-done = bf16[128,256]{1,0:T(8,128)(2,1)} async-done(((bf16[1024,256]{1,0:T(8,128)(2,1)}), bf16[128,256]{1,0:T(8,128)(2,1)}) %reduce-scatter.6.cloned.1.call-update) | async-done | bytes 65552 | tf_op jit(solution)/shard_map/while
  1348.7 19.6 %all_gather.26 = bf16[1,256,1024]{2,1,0:T(8,128)(2,1)S(1)} all-gather(bf16[1,256,128]{2,1,0:T(8,128)(2,1)S(1)} %get-tuple-element.1489), channel_id=1, replica_groups=mesh['dp'=4,'segment'=8,'chan'=8] {'chan'}, dimensions={2}, use_global_device_ids=true | all-gather | bytes 589824 | tf_op jit(solution)/shard_map/while/body/eval_jaxpr/all_gather | solution.py:158
  1368.4 27.5 %conditional.10 = (f32[9,1024,128]{2,1,0:T(8,128)}) conditional(s32[]{:T(128)} %convert_element_type.631, () %tuple.163, (bf16[1,256,1024]{2,1,0:T(8,128)(2,1)S(1)}, pred[]{:T(512)}, pred[]{:T(512)}, bf16[1,1,256,128]{3,2,1,0:T(8,128)(2,1)S(1)}, bf16[1,1,256,128]{3,2,1,0:T(8,128)(2,1)S(1)}, ...), branch_computations={%region_16.16_spmd, %region_17.17_spmd} | conditional | flops 604045312 | bytes 33226762 | solution.py:159
  1410.1 27.1 %reduce-scatter.6.cloned.1.call-done = bf16[128,256]{1,0:T(8,128)(2,1)} async-done(((bf16[1024,256]{1,0:T(8,128)(2,1)}), bf16[128,256]{1,0:T(8,128)(2,1)}) %reduce-scatter.6.cloned.1.call-update) | async-done | bytes 65552 | tf_op jit(solution)/shard_map/while
  1441.0 19.8 %all_gather.26 = bf16[1,256,1024]{2,1,0:T(8,128)(2,1)S(1)} all-gather(bf16[1,256,128]{2,1,0:T(8,128)(2,1)S(1)} %get-tuple-element.1489), channel_id=1, replica_groups=mesh['dp'=4,'segment'=8,'chan'=8] {'chan'}, dimensions={2}, use_global_device_ids=true | all-gather | bytes 589824 | tf_op jit(solution)/shard_map/while/body/eval_jaxpr/all_gather | solution.py:158
  1460.8 27.5 %conditional.10 = (f32[9,1024,128]{2,1,0:T(8,128)}) conditional(s32[]{:T(128)} %convert_element_type.631, () %tuple.163, (bf16[1,256,1024]{2,1,0:T(8,128)(2,1)S(1)}, pred[]{:T(512)}, pred[]{:T(512)}, bf16[1,1,256,128]{3,2,1,0:T(8,128)(2,1)S(1)}, bf16[1,1,256,128]{3,2,1,0:T(8,128)(2,1)S(1)}, ...), branch_computations={%region_16.16_spmd, %region_17.17_spmd} | conditional | flops 604045312 | bytes 33226762 | solution.py:159
  1500.6 8.8 all-reduce.3
  1510.4 51.4 %all-reduce.6.cloned.1.call-done = bf16[1,9,1024,128]{3,2,1,0:T(8,128)(2,1)} async-done(((bf16[1,9,1024,128]{3,2,1,0:T(8,128)(2,1)}), bf16[1,9,1024,128]{3,2,1,0:T(8,128)(2,1)}) %all-reduce.6.cloned.1.call-update) | async-done | bytes 2359312 | tf_op jit(solution)/shard_map/psum | solution.py:210
  (861 shorter events, 476.6 us)
Async XLA Ops:
  31.2 7.1 collective-permute-start
  59.0 9.6 collective-permute-start
  89.9 9.6 collective-permute-start
  120.7 9.6 collective-permute-start
  147.8 19.0 %collective-permute-start = (bf16[4,1,256,128]{3,2,1,0:T(8,128)(2,1)S(1)}, bf16[4,1,256,128]{3,2,1,0:T(8,128)(2,1)S(1)}, u32[]{:S(2)}, u32[]{:S(2)}) collective-permute-start(bf16[4,1,256,128]{3,2,1,0:T(8,128)(2,1)S(1)} %fusion.68), channel_id=1, source_target_pairs={{0,8},{8,16},{16,24},{24,32},{32,40},{40,48},{48,56},{1,9},{9,17},... | collective-permute-start | bytes 786440 | tf_op jit(solution)/shard_map/while/body/eval_jaxpr/ppermute | solution.py:14
  184.3 19.7 %collective-permute-start = (bf16[4,1,256,128]{3,2,1,0:T(8,128)(2,1)S(1)}, bf16[4,1,256,128]{3,2,1,0:T(8,128)(2,1)S(1)}, u32[]{:S(2)}, u32[]{:S(2)}) collective-permute-start(bf16[4,1,256,128]{3,2,1,0:T(8,128)(2,1)S(1)} %fusion.68), channel_id=1, source_target_pairs={{0,8},{8,16},{16,24},{24,32},{32,40},{40,48},{48,56},{1,9},{9,17},... | collective-permute-start | bytes 786440 | tf_op jit(solution)/shard_map/while/body/eval_jaxpr/ppermute | solution.py:14
  221.5 19.6 %collective-permute-start = (bf16[4,1,256,128]{3,2,1,0:T(8,128)(2,1)S(1)}, bf16[4,1,256,128]{3,2,1,0:T(8,128)(2,1)S(1)}, u32[]{:S(2)}, u32[]{:S(2)}) collective-permute-start(bf16[4,1,256,128]{3,2,1,0:T(8,128)(2,1)S(1)} %fusion.68), channel_id=1, source_target_pairs={{0,8},{8,16},{16,24},{24,32},{32,40},{40,48},{48,56},{1,9},{9,17},... | collective-permute-start | bytes 786440 | tf_op jit(solution)/shard_map/while/body/eval_jaxpr/ppermute | solution.py:14
  258.6 19.6 %collective-permute-start = (bf16[4,1,256,128]{3,2,1,0:T(8,128)(2,1)S(1)}, bf16[4,1,256,128]{3,2,1,0:T(8,128)(2,1)S(1)}, u32[]{:S(2)}, u32[]{:S(2)}) collective-permute-start(bf16[4,1,256,128]{3,2,1,0:T(8,128)(2,1)S(1)} %fusion.68), channel_id=1, source_target_pairs={{0,8},{8,16},{16,24},{24,32},{32,40},{40,48},{48,56},{1,9},{9,17},... | collective-permute-start | bytes 786440 | tf_op jit(solution)/shard_map/while/body/eval_jaxpr/ppermute | solution.py:14
  295.7 23.3 %collective-permute-start = (bf16[4,1,256,128]{3,2,1,0:T(8,128)(2,1)S(1)}, bf16[4,1,256,128]{3,2,1,0:T(8,128)(2,1)S(1)}, u32[]{:S(2)}, u32[]{:S(2)}) collective-permute-start(bf16[4,1,256,128]{3,2,1,0:T(8,128)(2,1)S(1)} %fusion.68), channel_id=1, source_target_pairs={{0,8},{8,16},{16,24},{24,32},{32,40},{40,48},{48,56},{1,9},{9,17},... | collective-permute-start | bytes 786440 | tf_op jit(solution)/shard_map/while/body/eval_jaxpr/ppermute | solution.py:14
  336.5 19.6 %collective-permute-start = (bf16[4,1,256,128]{3,2,1,0:T(8,128)(2,1)S(1)}, bf16[4,1,256,128]{3,2,1,0:T(8,128)(2,1)S(1)}, u32[]{:S(2)}, u32[]{:S(2)}) collective-permute-start(bf16[4,1,256,128]{3,2,1,0:T(8,128)(2,1)S(1)} %fusion.68), channel_id=1, source_target_pairs={{0,8},{8,16},{16,24},{24,32},{32,40},{40,48},{48,56},{1,9},{9,17},... | collective-permute-start | bytes 786440 | tf_op jit(solution)/shard_map/while/body/eval_jaxpr/ppermute | solution.py:14
  373.6 23.3 %collective-permute-start = (bf16[4,1,256,128]{3,2,1,0:T(8,128)(2,1)S(1)}, bf16[4,1,256,128]{3,2,1,0:T(8,128)(2,1)S(1)}, u32[]{:S(2)}, u32[]{:S(2)}) collective-permute-start(bf16[4,1,256,128]{3,2,1,0:T(8,128)(2,1)S(1)} %fusion.68), channel_id=1, source_target_pairs={{0,8},{8,16},{16,24},{24,32},{32,40},{40,48},{48,56},{1,9},{9,17},... | collective-permute-start | bytes 786440 | tf_op jit(solution)/shard_map/while/body/eval_jaxpr/ppermute | solution.py:14
  397.6 74.5 %copy-start.1 = (bf16[4,1,256,128]{3,2,1,0:T(8,128)(2,1)}, bf16[4,1,256,128]{3,2,1,0:T(8,128)(2,1)S(1)}, u32[]{:S(2)}) copy-start(bf16[4,1,256,128]{3,2,1,0:T(8,128)(2,1)S(1)} %get-tuple-element.1623) | copy-start | bytes 786436 | tf_op jit(solution)/shard_map/while
  397.6 72.6 %reduce-scatter.6.cloned.1.call-start = ((), (), s32[]{:S(2)}) async-start(), calls=%async_computation.2 | async-start | bytes 589824 | tf_op jit(solution)/shard_map/while
  398.7 72.5 %copy-start.3 = (f32[1,128]{1,0:T(1,128)S(1)}, f32[1,128]{1,0:T(1,128)}, u32[]{:S(2)}) copy-start(f32[1,128]{1,0:T(1,128)} %get-tuple-element.1625) | copy-start | bytes 1540 | tf_op jit(solution)/shard_map/while
  398.7 72.5 %copy-start.4 = (f32[1,128]{1,0:T(1,128)S(1)}, f32[1,128]{1,0:T(1,128)}, u32[]{:S(2)}) copy-start(f32[1,128]{1,0:T(1,128)} %get-tuple-element.1626) | copy-start | bytes 1540 | tf_op jit(solution)/shard_map/while
  472.8 28.4 %collective-permute-start.1 = (bf16[4,1,256,128]{3,2,1,0:T(8,128)(2,1)}, bf16[4,1,256,128]{3,2,1,0:T(8,128)(2,1)}, u32[]{:S(2)}, u32[]{:S(2)}) collective-permute-start(bf16[4,1,256,128]{3,2,1,0:T(8,128)(2,1)} %fusion.72), channel_id=1, source_target_pairs={{8,0},{16,8},{24,16},{32,24},{40,32},{48,40},{56,48},{9,1},{17,9},... | collective-permute-start | bytes 786440 | tf_op jit(solution)/shard_map/while/body/eval_jaxpr/ppermute | solution.py:14
  502.9 62.2 %reduce-scatter.6.cloned.1.call-start = ((), (), s32[]{:S(2)}) async-start(), calls=%async_computation.2 | async-start | bytes 589824 | tf_op jit(solution)/shard_map/while
  567.7 29.8 %collective-permute-start.1 = (bf16[4,1,256,128]{3,2,1,0:T(8,128)(2,1)}, bf16[4,1,256,128]{3,2,1,0:T(8,128)(2,1)}, u32[]{:S(2)}, u32[]{:S(2)}) collective-permute-start(bf16[4,1,256,128]{3,2,1,0:T(8,128)(2,1)} %fusion.72), channel_id=1, source_target_pairs={{8,0},{16,8},{24,16},{32,24},{40,32},{48,40},{56,48},{9,1},{17,9},... | collective-permute-start | bytes 786440 | tf_op jit(solution)/shard_map/while/body/eval_jaxpr/ppermute | solution.py:14
  599.2 62.0 %reduce-scatter.6.cloned.1.call-start = ((), (), s32[]{:S(2)}) async-start(), calls=%async_computation.2 | async-start | bytes 589824 | tf_op jit(solution)/shard_map/while
  663.8 29.9 %collective-permute-start.1 = (bf16[4,1,256,128]{3,2,1,0:T(8,128)(2,1)}, bf16[4,1,256,128]{3,2,1,0:T(8,128)(2,1)}, u32[]{:S(2)}, u32[]{:S(2)}) collective-permute-start(bf16[4,1,256,128]{3,2,1,0:T(8,128)(2,1)} %fusion.72), channel_id=1, source_target_pairs={{8,0},{16,8},{24,16},{32,24},{40,32},{48,40},{56,48},{9,1},{17,9},... | collective-permute-start | bytes 786440 | tf_op jit(solution)/shard_map/while/body/eval_jaxpr/ppermute | solution.py:14
  695.4 62.1 %reduce-scatter.6.cloned.1.call-start = ((), (), s32[]{:S(2)}) async-start(), calls=%async_computation.2 | async-start | bytes 589824 | tf_op jit(solution)/shard_map/while
  760.1 29.9 %collective-permute-start.1 = (bf16[4,1,256,128]{3,2,1,0:T(8,128)(2,1)}, bf16[4,1,256,128]{3,2,1,0:T(8,128)(2,1)}, u32[]{:S(2)}, u32[]{:S(2)}) collective-permute-start(bf16[4,1,256,128]{3,2,1,0:T(8,128)(2,1)} %fusion.72), channel_id=1, source_target_pairs={{8,0},{16,8},{24,16},{32,24},{40,32},{48,40},{56,48},{9,1},{17,9},... | collective-permute-start | bytes 786440 | tf_op jit(solution)/shard_map/while/body/eval_jaxpr/ppermute | solution.py:14
  791.8 68.6 %copy-start.1 = (bf16[4,1,256,128]{3,2,1,0:T(8,128)(2,1)}, bf16[4,1,256,128]{3,2,1,0:T(8,128)(2,1)S(1)}, u32[]{:S(2)}) copy-start(bf16[4,1,256,128]{3,2,1,0:T(8,128)(2,1)S(1)} %get-tuple-element.1623) | copy-start | bytes 786436 | tf_op jit(solution)/shard_map/while
  791.8 66.7 %reduce-scatter.6.cloned.1.call-start = ((), (), s32[]{:S(2)}) async-start(), calls=%async_computation.2 | async-start | bytes 589824 | tf_op jit(solution)/shard_map/while
  792.8 66.7 %copy-start.3 = (f32[1,128]{1,0:T(1,128)S(1)}, f32[1,128]{1,0:T(1,128)}, u32[]{:S(2)}) copy-start(f32[1,128]{1,0:T(1,128)} %get-tuple-element.1625) | copy-start | bytes 1540 | tf_op jit(solution)/shard_map/while
  792.9 66.7 %copy-start.4 = (f32[1,128]{1,0:T(1,128)S(1)}, f32[1,128]{1,0:T(1,128)}, u32[]{:S(2)}) copy-start(f32[1,128]{1,0:T(1,128)} %get-tuple-element.1626) | copy-start | bytes 1540 | tf_op jit(solution)/shard_map/while
  861.1 30.1 %collective-permute-start.1 = (bf16[4,1,256,128]{3,2,1,0:T(8,128)(2,1)}, bf16[4,1,256,128]{3,2,1,0:T(8,128)(2,1)}, u32[]{:S(2)}, u32[]{:S(2)}) collective-permute-start(bf16[4,1,256,128]{3,2,1,0:T(8,128)(2,1)} %fusion.72), channel_id=1, source_target_pairs={{8,0},{16,8},{24,16},{32,24},{40,32},{48,40},{56,48},{9,1},{17,9},... | collective-permute-start | bytes 786440 | tf_op jit(solution)/shard_map/while/body/eval_jaxpr/ppermute | solution.py:14
  892.8 68.7 %copy-start.1 = (bf16[4,1,256,128]{3,2,1,0:T(8,128)(2,1)}, bf16[4,1,256,128]{3,2,1,0:T(8,128)(2,1)S(1)}, u32[]{:S(2)}) copy-start(bf16[4,1,256,128]{3,2,1,0:T(8,128)(2,1)S(1)} %get-tuple-element.1623) | copy-start | bytes 786436 | tf_op jit(solution)/shard_map/while
  892.8 66.7 %reduce-scatter.6.cloned.1.call-start = ((), (), s32[]{:S(2)}) async-start(), calls=%async_computation.2 | async-start | bytes 589824 | tf_op jit(solution)/shard_map/while
  893.9 66.7 %copy-start.3 = (f32[1,128]{1,0:T(1,128)S(1)}, f32[1,128]{1,0:T(1,128)}, u32[]{:S(2)}) copy-start(f32[1,128]{1,0:T(1,128)} %get-tuple-element.1625) | copy-start | bytes 1540 | tf_op jit(solution)/shard_map/while
  893.9 66.7 %copy-start.4 = (f32[1,128]{1,0:T(1,128)S(1)}, f32[1,128]{1,0:T(1,128)}, u32[]{:S(2)}) copy-start(f32[1,128]{1,0:T(1,128)} %get-tuple-element.1626) | copy-start | bytes 1540 | tf_op jit(solution)/shard_map/while
  962.2 29.8 %collective-permute-start.1 = (bf16[4,1,256,128]{3,2,1,0:T(8,128)(2,1)}, bf16[4,1,256,128]{3,2,1,0:T(8,128)(2,1)}, u32[]{:S(2)}, u32[]{:S(2)}) collective-permute-start(bf16[4,1,256,128]{3,2,1,0:T(8,128)(2,1)} %fusion.72), channel_id=1, source_target_pairs={{8,0},{16,8},{24,16},{32,24},{40,32},{48,40},{56,48},{9,1},{17,9},... | collective-permute-start | bytes 786440 | tf_op jit(solution)/shard_map/while/body/eval_jaxpr/ppermute | solution.py:14
  993.7 68.6 %copy-start.1 = (bf16[4,1,256,128]{3,2,1,0:T(8,128)(2,1)}, bf16[4,1,256,128]{3,2,1,0:T(8,128)(2,1)S(1)}, u32[]{:S(2)}) copy-start(bf16[4,1,256,128]{3,2,1,0:T(8,128)(2,1)S(1)} %get-tuple-element.1623) | copy-start | bytes 786436 | tf_op jit(solution)/shard_map/while
  993.7 66.7 %reduce-scatter.6.cloned.1.call-start = ((), (), s32[]{:S(2)}) async-start(), calls=%async_computation.2 | async-start | bytes 589824 | tf_op jit(solution)/shard_map/while
  994.8 66.6 %copy-start.3 = (f32[1,128]{1,0:T(1,128)S(1)}, f32[1,128]{1,0:T(1,128)}, u32[]{:S(2)}) copy-start(f32[1,128]{1,0:T(1,128)} %get-tuple-element.1625) | copy-start | bytes 1540 | tf_op jit(solution)/shard_map/while
  994.8 66.6 %copy-start.4 = (f32[1,128]{1,0:T(1,128)S(1)}, f32[1,128]{1,0:T(1,128)}, u32[]{:S(2)}) copy-start(f32[1,128]{1,0:T(1,128)} %get-tuple-element.1626) | copy-start | bytes 1540 | tf_op jit(solution)/shard_map/while
  1063.0 29.9 %collective-permute-start.1 = (bf16[4,1,256,128]{3,2,1,0:T(8,128)(2,1)}, bf16[4,1,256,128]{3,2,1,0:T(8,128)(2,1)}, u32[]{:S(2)}, u32[]{:S(2)}) collective-permute-start(bf16[4,1,256,128]{3,2,1,0:T(8,128)(2,1)} %fusion.72), channel_id=1, source_target_pairs={{8,0},{16,8},{24,16},{32,24},{40,32},{48,40},{56,48},{9,1},{17,9},... | collective-permute-start | bytes 786440 | tf_op jit(solution)/shard_map/while/body/eval_jaxpr/ppermute | solution.py:14
  1094.6 66.3 %copy-start.1 = (bf16[4,1,256,128]{3,2,1,0:T(8,128)(2,1)}, bf16[4,1,256,128]{3,2,1,0:T(8,128)(2,1)S(1)}, u32[]{:S(2)}) copy-start(bf16[4,1,256,128]{3,2,1,0:T(8,128)(2,1)S(1)} %get-tuple-element.1623) | copy-start | bytes 786436 | tf_op jit(solution)/shard_map/while
  1094.6 64.3 %reduce-scatter.6.cloned.1.call-start = ((), (), s32[]{:S(2)}) async-start(), calls=%async_computation.2 | async-start | bytes 589824 | tf_op jit(solution)/shard_map/while
  1095.7 64.3 %copy-start.3 = (f32[1,128]{1,0:T(1,128)S(1)}, f32[1,128]{1,0:T(1,128)}, u32[]{:S(2)}) copy-start(f32[1,128]{1,0:T(1,128)} %get-tuple-element.1625) | copy-start | bytes 1540 | tf_op jit(solution)/shard_map/while
  1161.6 54.7 %collective-permute-start.1 = (bf16[4,1,256,128]{3,2,1,0:T(8,128)(2,1)}, bf16[4,1,256,128]{3,2,1,0:T(8,128)(2,1)}, u32[]{:S(2)}, u32[]{:S(2)}) collective-permute-start(bf16[4,1,256,128]{3,2,1,0:T(8,128)(2,1)} %fusion.72), channel_id=1, source_target_pairs={{8,0},{16,8},{24,16},{32,24},{40,32},{48,40},{56,48},{9,1},{17,9},... | collective-permute-start | bytes 786440 | tf_op jit(solution)/shard_map/while/body/eval_jaxpr/ppermute | solution.py:14
  1218.0 34.5 %reduce-scatter.6.cloned.1.call-start = ((), (), s32[]{:S(2)}) async-start(), calls=%async_computation.2 | async-start | bytes 589824 | tf_op jit(solution)/shard_map/while
  1255.1 54.9 %collective-permute-start.1 = (bf16[4,1,256,128]{3,2,1,0:T(8,128)(2,1)}, bf16[4,1,256,128]{3,2,1,0:T(8,128)(2,1)}, u32[]{:S(2)}, u32[]{:S(2)}) collective-permute-start(bf16[4,1,256,128]{3,2,1,0:T(8,128)(2,1)} %fusion.72), channel_id=1, source_target_pairs={{8,0},{16,8},{24,16},{32,24},{40,32},{48,40},{56,48},{9,1},{17,9},... | collective-permute-start | bytes 786440 | tf_op jit(solution)/shard_map/while/body/eval_jaxpr/ppermute | solution.py:14
  1311.7 33.1 %reduce-scatter.6.cloned.1.call-start = ((), (), s32[]{:S(2)}) async-start(), calls=%async_computation.2 | async-start | bytes 589824 | tf_op jit(solution)/shard_map/while
  1347.5 54.9 %collective-permute-start.1 = (bf16[4,1,256,128]{3,2,1,0:T(8,128)(2,1)}, bf16[4,1,256,128]{3,2,1,0:T(8,128)(2,1)}, u32[]{:S(2)}, u32[]{:S(2)}) collective-permute-start(bf16[4,1,256,128]{3,2,1,0:T(8,128)(2,1)} %fusion.72), channel_id=1, source_target_pairs={{8,0},{16,8},{24,16},{32,24},{40,32},{48,40},{56,48},{9,1},{17,9},... | collective-permute-start | bytes 786440 | tf_op jit(solution)/shard_map/while/body/eval_jaxpr/ppermute | solution.py:14
  1404.0 33.1 %reduce-scatter.6.cloned.1.call-start = ((), (), s32[]{:S(2)}) async-start(), calls=%async_computation.2 | async-start | bytes 589824 | tf_op jit(solution)/shard_map/while
  1439.7 55.1 %collective-permute-start.1 = (bf16[4,1,256,128]{3,2,1,0:T(8,128)(2,1)}, bf16[4,1,256,128]{3,2,1,0:T(8,128)(2,1)}, u32[]{:S(2)}, u32[]{:S(2)}) collective-permute-start(bf16[4,1,256,128]{3,2,1,0:T(8,128)(2,1)} %fusion.72), channel_id=1, source_target_pairs={{8,0},{16,8},{24,16},{32,24},{40,32},{48,40},{56,48},{9,1},{17,9},... | collective-permute-start | bytes 786440 | tf_op jit(solution)/shard_map/while/body/eval_jaxpr/ppermute | solution.py:14
  1496.5 65.3 %all-reduce.6.cloned.1.call-start = ((), (), s32[]{:S(2)}) async-start(), calls=%async_computation.1 | async-start | bytes 4718592 | tf_op jit(solution)/shard_map/psum | solution.py:210
  (34 other events, 1031.6 us)
Sparse Core Ops, SparseCore 0:
  400.9 69.1 reduce-scatter.5
  506.2 58.8 reduce-scatter.5
  602.5 58.6 reduce-scatter.5
  698.5 58.9 reduce-scatter.5
  794.8 63.5 reduce-scatter.5
  895.9 63.5 reduce-scatter.5
  997.0 63.3 reduce-scatter.5
  1100.4 58.4 reduce-scatter.5
  1223.8 28.6 reduce-scatter.5
  1317.5 27.2 reduce-scatter.5
  1409.8 27.2 reduce-scatter.5
Sparse Core Ops, SparseCore 1:
  1500.7 61.0 all-reduce.5
where the time goes:
time: 1580 us; the launch traced here: 1570 us
  waiting for transfers between devices  688 us (44%)
  blocking collectives  389 us (25%)
  local copies, waits for them, and re-layouts  178 us (11%)
  starting transfers between devices  133 us (8%)
  other arithmetic  126 us (8%)
  matrix products  39.6 us (3%)
    while x22, waiting for transfers between devices  577 us
    all_gather x11, blocking collectives, backward_tick(): shard_piece = lax.all_gather(hidden, 'chan', axis=2, tiled=True)  216 us
    all_gather x11, blocking collectives, forward_tick(): shard_piece = lax.all_gather(hidden, 'chan', axis=2, tiled=True)  165 us
    ppermute x22, starting transfers between devices, shifted(): return lax.ppermute(shard, axis, pairs)  133 us
    add x11, other arithmetic, backward_tick(): grad_weight + lax.cond(active, lambda: jnp.einsum('trc,ro->tco', shifted_...  69.6 us
    ppermute x22, waiting for transfers between devices, shifted(): return lax.ppermute(shard, axis, pairs)  60.2 us
    psum x1, waiting for transfers between devices, local(): lax.psum(backward_state[1].astype(jnp.bfloat16), 'dp').astype(jnp.float32)  51.4 us
    cond x104, local copies, waits for them, and re-layouts  50.2 us
  transfers between devices with their start and end apart: 34, of which 23 were waited for; matrix products, arithmetic and copies ran while one was open for 13% of the time, Pallas kernels for 0%

commit v1 on v0

--- a/solution.py
+++ b/solution.py
@@ -1,3 +1,4 @@
+import functools
 import jax
 import jax.numpy as jnp
 from jax import lax
@@ -6,6 +7,17 @@
 GROUPS = 32
 SIDE = 16
 EPSILON = 1e-05
+
+
+def _find_results(row_data, link_axis):
+    then = lax.axis_size(link_axis)
+    kept_arr = jnp.stack(then * [row_data], axis=0)
+    m_next = lax.all_to_all(kept_arr, link_axis, 0, 0)
+    part_now = jnp.concatenate(m_next, axis=2)
+    return part_now
+
+
+balance_the_squares = functools.partial(_find_results, link_axis="chan")
 
 
 def shifted(shard, axis, by):
@@ -155,7 +167,7 @@
         sigma = jax.nn.sigmoid(pre_act)
         grad_rows = grad_out.reshape(row_count, local_width)
         hidden = (pre_act * sigma).astype(jnp.bfloat16)
-        shard_piece = lax.all_gather(hidden, "chan", axis=2, tiled=True)
+        shard_piece = balance_the_squares(hidden)
         grad_weight = grad_weight + lax.cond(
             active,
             lambda: jnp.einsum(

time: 1580 us -> 1320 us (0.84)
  blocking collectives: 389 us -> 172 us
  waiting for transfers between devices: 688 us -> 557 us
  starting transfers between devices: 133 us -> 209 us
    while x22, waiting for transfers between devices: 577 us -> 242 us
    all_gather x11 -> x0, blocking collectives: 216 us -> none  [backward_tick(): shard_piece = lax.all_gather(hidden, 'chan', axis=2, tiled=True)]
    all_to_all x0 -> x11, waiting for transfers between devices: none -> 178 us  [_find_results(): m_next = lax.all_to_all(kept_arr, link_axis, 0, 0)]
    all_to_all x0 -> x11, starting transfers between devices: none -> 75.6 us  [_find_results(): m_next = lax.all_to_all(kept_arr, link_axis, 0, 0)]
    ppermute x22, waiting for transfers between devices: 60.2 us -> 84.7 us  [shifted(): return lax.ppermute(shard, axis, pairs)]
    while x154 -> x308, local copies, waits for them, and re-layouts: 49.4 us -> 34.5 us
    cond x104 -> x120, local copies, waits for them, and re-layouts: 50.2 us -> 49.9 us
  transfers between devices with their start and end apart: 34 -> 45, of which waited for: 23 -> 36; matrix products, arithmetic and copies ran while one was open for 13% -> 17% of each run, Pallas kernels for 0% -> 0%
where the time goes in v1:
time: 1320 us
  waiting for transfers between devices  557 us (42%)
  starting transfers between devices  209 us (16%)
  local copies, waits for them, and re-layouts  191 us (14%)
  blocking collectives  172 us (13%)
  other arithmetic  131 us (10%)
  matrix products  39.6 us (3%)
  between operations  15.3 us (1%)
    while x22, waiting for transfers between devices  242 us
    all_to_all x11, waiting for transfers between devices, _find_results(): m_next = lax.all_to_all(kept_arr, link_axis, 0, 0)  178 us
    all_gather x11, blocking collectives, forward_tick(): shard_piece = lax.all_gather(hidden, 'chan', axis=2, tiled=True)  165 us
    ppermute x22, starting transfers between devices, shifted(): return lax.ppermute(shard, axis, pairs)  133 us
    ppermute x22, waiting for transfers between devices, shifted(): return lax.ppermute(shard, axis, pairs)  84.7 us
    all_to_all x11, starting transfers between devices, _find_results(): m_next = lax.all_to_all(kept_arr, link_axis, 0, 0)  75.6 us
    add x11, other arithmetic, backward_tick(): grad_weight + lax.cond(active, lambda: jnp.einsum('trc,ro->tco', shifted_...  69.3 us
    psum x1, waiting for transfers between devices, local(): lax.psum(backward_state[1].astype(jnp.bfloat16), 'dp').astype(jnp.float32)  52.7 us
  transfers between devices with their start and end apart: 45, of which 36 were waited for; matrix products, arithmetic and copies ran while one was open for 17% of the time, Pallas kernels for 0%

profile of v1, /device:TPU:1, one launch (start us, length us, event | category | flops | bytes accessed | tf_op | source)
XLA Modules:
  0.0 1319.4 jit_solution(3413243918233360718)
XLA Ops:
  8.2 388.7 %while.47 = (s32[]{:T(128)}, bf16[4,1,256,128]{3,2,1,0:T(8,128)(2,1)S(1)}, bf16[4,1,256,128]{3,2,1,0:T(8,128)(2,1)S(1)}, f32[4,1,4]{2,1,0:T(1,128)S(1)}, f32[4,1...) while((s32[]{:T(128)}, ...), condition=%wide.region_7.8_spmd, body=%wide.region_0.7_spmd.sunk | while | flops 604864512 | bytes 33960956 | solution.py:139
  10.7 16.7 %all_gather.12 = bf16[1,256,1024]{2,1,0:T(8,128)(2,1)S(1)} all-gather(bf16[1,256,128]{2,1,0:T(8,128)(2,1)S(1)} %fusion.77), channel_id=1, replica_groups=mesh['dp'=4,'segment'=8,'chan'=8] {'chan'}, dimensions={2}, use_global_device_ids=true | all-gather | bytes 589824 | tf_op jit(solution)/shard_map/while/body/eval_jaxpr/all_gather | solution.py:115
  40.8 14.4 %all_gather.12 = bf16[1,256,1024]{2,1,0:T(8,128)(2,1)S(1)} all-gather(bf16[1,256,128]{2,1,0:T(8,128)(2,1)S(1)} %fusion.77), channel_id=1, replica_groups=mesh['dp'=4,'segment'=8,'chan'=8] {'chan'}, dimensions={2}, use_global_device_ids=true | all-gather | bytes 589824 | tf_op jit(solution)/shard_map/while/body/eval_jaxpr/all_gather | solution.py:115
  71.2 14.9 %all_gather.12 = bf16[1,256,1024]{2,1,0:T(8,128)(2,1)S(1)} all-gather(bf16[1,256,128]{2,1,0:T(8,128)(2,1)S(1)} %fusion.77), channel_id=1, replica_groups=mesh['dp'=4,'segment'=8,'chan'=8] {'chan'}, dimensions={2}, use_global_device_ids=true | all-gather | bytes 589824 | tf_op jit(solution)/shard_map/while/body/eval_jaxpr/all_gather | solution.py:115
  102.1 14.9 %all_gather.12 = bf16[1,256,1024]{2,1,0:T(8,128)(2,1)S(1)} all-gather(bf16[1,256,128]{2,1,0:T(8,128)(2,1)S(1)} %fusion.77), channel_id=1, replica_groups=mesh['dp'=4,'segment'=8,'chan'=8] {'chan'}, dimensions={2}, use_global_device_ids=true | all-gather | bytes 589824 | tf_op jit(solution)/shard_map/while/body/eval_jaxpr/all_gather | solution.py:115
  132.9 14.9 %all_gather.12 = bf16[1,256,1024]{2,1,0:T(8,128)(2,1)S(1)} all-gather(bf16[1,256,128]{2,1,0:T(8,128)(2,1)S(1)} %fusion.77), channel_id=1, replica_groups=mesh['dp'=4,'segment'=8,'chan'=8] {'chan'}, dimensions={2}, use_global_device_ids=true | all-gather | bytes 589824 | tf_op jit(solution)/shard_map/while/body/eval_jaxpr/all_gather | solution.py:115
  147.9 13.5 %collective-permute-start = (bf16[4,1,256,128]{3,2,1,0:T(8,128)(2,1)S(1)}, bf16[4,1,256,128]{3,2,1,0:T(8,128)(2,1)S(1)}, u32[]{:S(2)}, u32[]{:S(2)}) collective-permute-start(bf16[4,1,256,128]{3,2,1,0:T(8,128)(2,1)S(1)} %fusion.78), channel_id=1, source_target_pairs={{0,8},{8,16},{16,24},{24,32},{32,40},{40,48},{48,56},{1,9},{9,17},... | collective-permute-start | bytes 786440 | tf_op jit(solution)/shard_map/while/body/eval_jaxpr/ppermute | solution.py:26
  169.4 14.9 %all_gather.12 = bf16[1,256,1024]{2,1,0:T(8,128)(2,1)S(1)} all-gather(bf16[1,256,128]{2,1,0:T(8,128)(2,1)S(1)} %fusion.77), channel_id=1, replica_groups=mesh['dp'=4,'segment'=8,'chan'=8] {'chan'}, dimensions={2}, use_global_device_ids=true | all-gather | bytes 589824 | tf_op jit(solution)/shard_map/while/body/eval_jaxpr/all_gather | solution.py:115
  184.4 14.2 %collective-permute-start = (bf16[4,1,256,128]{3,2,1,0:T(8,128)(2,1)S(1)}, bf16[4,1,256,128]{3,2,1,0:T(8,128)(2,1)S(1)}, u32[]{:S(2)}, u32[]{:S(2)}) collective-permute-start(bf16[4,1,256,128]{3,2,1,0:T(8,128)(2,1)S(1)} %fusion.78), channel_id=1, source_target_pairs={{0,8},{8,16},{16,24},{24,32},{32,40},{40,48},{48,56},{1,9},{9,17},... | collective-permute-start | bytes 786440 | tf_op jit(solution)/shard_map/while/body/eval_jaxpr/ppermute | solution.py:26
  206.6 14.9 %all_gather.12 = bf16[1,256,1024]{2,1,0:T(8,128)(2,1)S(1)} all-gather(bf16[1,256,128]{2,1,0:T(8,128)(2,1)S(1)} %fusion.77), channel_id=1, replica_groups=mesh['dp'=4,'segment'=8,'chan'=8] {'chan'}, dimensions={2}, use_global_device_ids=true | all-gather | bytes 589824 | tf_op jit(solution)/shard_map/while/body/eval_jaxpr/all_gather | solution.py:115
  221.5 14.1 %collective-permute-start = (bf16[4,1,256,128]{3,2,1,0:T(8,128)(2,1)S(1)}, bf16[4,1,256,128]{3,2,1,0:T(8,128)(2,1)S(1)}, u32[]{:S(2)}, u32[]{:S(2)}) collective-permute-start(bf16[4,1,256,128]{3,2,1,0:T(8,128)(2,1)S(1)} %fusion.78), channel_id=1, source_target_pairs={{0,8},{8,16},{16,24},{24,32},{32,40},{40,48},{48,56},{1,9},{9,17},... | collective-permute-start | bytes 786440 | tf_op jit(solution)/shard_map/while/body/eval_jaxpr/ppermute | solution.py:26
  243.7 14.9 %all_gather.12 = bf16[1,256,1024]{2,1,0:T(8,128)(2,1)S(1)} all-gather(bf16[1,256,128]{2,1,0:T(8,128)(2,1)S(1)} %fusion.77), channel_id=1, replica_groups=mesh['dp'=4,'segment'=8,'chan'=8] {'chan'}, dimensions={2}, use_global_device_ids=true | all-gather | bytes 589824 | tf_op jit(solution)/shard_map/while/body/eval_jaxpr/all_gather | solution.py:115
  258.6 14.1 %collective-permute-start = (bf16[4,1,256,128]{3,2,1,0:T(8,128)(2,1)S(1)}, bf16[4,1,256,128]{3,2,1,0:T(8,128)(2,1)S(1)}, u32[]{:S(2)}, u32[]{:S(2)}) collective-permute-start(bf16[4,1,256,128]{3,2,1,0:T(8,128)(2,1)S(1)} %fusion.78), channel_id=1, source_target_pairs={{0,8},{8,16},{16,24},{24,32},{32,40},{40,48},{48,56},{1,9},{9,17},... | collective-permute-start | bytes 786440 | tf_op jit(solution)/shard_map/while/body/eval_jaxpr/ppermute | solution.py:26
  280.8 14.9 %all_gather.12 = bf16[1,256,1024]{2,1,0:T(8,128)(2,1)S(1)} all-gather(bf16[1,256,128]{2,1,0:T(8,128)(2,1)S(1)} %fusion.77), channel_id=1, replica_groups=mesh['dp'=4,'segment'=8,'chan'=8] {'chan'}, dimensions={2}, use_global_device_ids=true | all-gather | bytes 589824 | tf_op jit(solution)/shard_map/while/body/eval_jaxpr/all_gather | solution.py:115
  295.7 17.8 %collective-permute-start = (bf16[4,1,256,128]{3,2,1,0:T(8,128)(2,1)S(1)}, bf16[4,1,256,128]{3,2,1,0:T(8,128)(2,1)S(1)}, u32[]{:S(2)}, u32[]{:S(2)}) collective-permute-start(bf16[4,1,256,128]{3,2,1,0:T(8,128)(2,1)S(1)} %fusion.78), channel_id=1, source_target_pairs={{0,8},{8,16},{16,24},{24,32},{32,40},{40,48},{48,56},{1,9},{9,17},... | collective-permute-start | bytes 786440 | tf_op jit(solution)/shard_map/while/body/eval_jaxpr/ppermute | solution.py:26
  321.6 14.9 %all_gather.12 = bf16[1,256,1024]{2,1,0:T(8,128)(2,1)S(1)} all-gather(bf16[1,256,128]{2,1,0:T(8,128)(2,1)S(1)} %fusion.77), channel_id=1, replica_groups=mesh['dp'=4,'segment'=8,'chan'=8] {'chan'}, dimensions={2}, use_global_device_ids=true | all-gather | bytes 589824 | tf_op jit(solution)/shard_map/while/body/eval_jaxpr/all_gather | solution.py:115
  336.5 14.1 %collective-permute-start = (bf16[4,1,256,128]{3,2,1,0:T(8,128)(2,1)S(1)}, bf16[4,1,256,128]{3,2,1,0:T(8,128)(2,1)S(1)}, u32[]{:S(2)}, u32[]{:S(2)}) collective-permute-start(bf16[4,1,256,128]{3,2,1,0:T(8,128)(2,1)S(1)} %fusion.78), channel_id=1, source_target_pairs={{0,8},{8,16},{16,24},{24,32},{32,40},{40,48},{48,56},{1,9},{9,17},... | collective-permute-start | bytes 786440 | tf_op jit(solution)/shard_map/while/body/eval_jaxpr/ppermute | solution.py:26
  358.6 14.9 %all_gather.12 = bf16[1,256,1024]{2,1,0:T(8,128)(2,1)S(1)} all-gather(bf16[1,256,128]{2,1,0:T(8,128)(2,1)S(1)} %fusion.77), channel_id=1, replica_groups=mesh['dp'=4,'segment'=8,'chan'=8] {'chan'}, dimensions={2}, use_global_device_ids=true | all-gather | bytes 589824 | tf_op jit(solution)/shard_map/while/body/eval_jaxpr/all_gather | solution.py:115
  373.6 17.8 %collective-permute-start = (bf16[4,1,256,128]{3,2,1,0:T(8,128)(2,1)S(1)}, bf16[4,1,256,128]{3,2,1,0:T(8,128)(2,1)S(1)}, u32[]{:S(2)}, u32[]{:S(2)}) collective-permute-start(bf16[4,1,256,128]{3,2,1,0:T(8,128)(2,1)S(1)} %fusion.78), channel_id=1, source_target_pairs={{0,8},{8,16},{16,24},{24,32},{32,40},{40,48},{48,56},{1,9},{9,17},... | collective-permute-start | bytes 786440 | tf_op jit(solution)/shard_map/while/body/eval_jaxpr/ppermute | solution.py:26
  397.0 845.7 %while.48 = (s32[]{:T(128)}, bf16[4,1,256,128]{3,2,1,0:T(8,128)(2,1)S(1)}, f32[9,1024,128]{2,1,0:T(8,128)}, f32[128]{0:T(128)}, f32[128]{0:T(128)}, /*index=5*/p...) while((s32[]{:T(128)}, ...), condition=%wide.region_20.21_spmd.clone, body=%wide.region_8.20_spmd.clone.sunk | while | flops 1211990528 | bytes 65440856 | solution.py:220
  406.1 14.4 %all-to-all-done = bf16[8,1,256,128]{3,2,1,0:T(8,128)(2,1)S(1)} async-done(((bf16[8,1,256,128]{3,2,1,0:T(8,128)(2,1)}), bf16[8,1,256,128]{3,2,1,0:T(8,128)(2,1)S(1)}, u32[]{:S(2)}, u32[]{:S(2)}) %all-to-all-start) | async-done | bytes 524320 | tf_op jit(solution)/shard_map/while/body/eval_jaxpr/all_to_all | solution.py:15
  423.1 46.8 %reduce-scatter.6.cloned.1.call-done = bf16[128,256]{1,0:T(8,128)(2,1)} async-done(((bf16[1024,256]{1,0:T(8,128)(2,1)}), bf16[128,256]{1,0:T(8,128)(2,1)}) %reduce-scatter.6.cloned.1.call-update) | async-done | bytes 65552 | tf_op jit(solution)/shard_map/while
  484.6 8.5 all-to-all-start
  493.1 14.4 %all-to-all-done = bf16[8,1,256,128]{3,2,1,0:T(8,128)(2,1)S(1)} async-done(((bf16[8,1,256,128]{3,2,1,0:T(8,128)(2,1)}), bf16[8,1,256,128]{3,2,1,0:T(8,128)(2,1)S(1)}, u32[]{:S(2)}, u32[]{:S(2)}) %all-to-all-start) | async-done | bytes 524320 | tf_op jit(solution)/shard_map/while/body/eval_jaxpr/all_to_all | solution.py:15
  510.0 17.9 %reduce-scatter.6.cloned.1.call-done = bf16[128,256]{1,0:T(8,128)(2,1)} async-done(((bf16[1024,256]{1,0:T(8,128)(2,1)}), bf16[128,256]{1,0:T(8,128)(2,1)}) %reduce-scatter.6.cloned.1.call-update) | async-done | bytes 65552 | tf_op jit(solution)/shard_map/while
  543.6 7.7 all-to-all-start
  551.3 14.4 %all-to-all-done = bf16[8,1,256,128]{3,2,1,0:T(8,128)(2,1)S(1)} async-done(((bf16[8,1,256,128]{3,2,1,0:T(8,128)(2,1)}), bf16[8,1,256,128]{3,2,1,0:T(8,128)(2,1)S(1)}, u32[]{:S(2)}, u32[]{:S(2)}) %all-to-all-start) | async-done | bytes 524320 | tf_op jit(solution)/shard_map/while/body/eval_jaxpr/all_to_all | solution.py:15
  568.2 26.9 %reduce-scatter.6.cloned.1.call-done = bf16[128,256]{1,0:T(8,128)(2,1)} async-done(((bf16[1024,256]{1,0:T(8,128)(2,1)}), bf16[128,256]{1,0:T(8,128)(2,1)}) %reduce-scatter.6.cloned.1.call-update) | async-done | bytes 65552 | tf_op jit(solution)/shard_map/while
  618.4 14.4 %all-to-all-done = bf16[8,1,256,128]{3,2,1,0:T(8,128)(2,1)S(1)} async-done(((bf16[8,1,256,128]{3,2,1,0:T(8,128)(2,1)}), bf16[8,1,256,128]{3,2,1,0:T(8,128)(2,1)S(1)}, u32[]{:S(2)}, u32[]{:S(2)}) %all-to-all-start) | async-done | bytes 524320 | tf_op jit(solution)/shard_map/while/body/eval_jaxpr/all_to_all | solution.py:15
  635.3 32.5 %reduce-scatter.6.cloned.1.call-done = bf16[128,256]{1,0:T(8,128)(2,1)} async-done(((bf16[1024,256]{1,0:T(8,128)(2,1)}), bf16[128,256]{1,0:T(8,128)(2,1)}) %reduce-scatter.6.cloned.1.call-update) | async-done | bytes 65552 | tf_op jit(solution)/shard_map/while
  690.7 20.0 %all-to-all-done = bf16[8,1,256,128]{3,2,1,0:T(8,128)(2,1)S(1)} async-done(((bf16[8,1,256,128]{3,2,1,0:T(8,128)(2,1)}), bf16[8,1,256,128]{3,2,1,0:T(8,128)(2,1)S(1)}, u32[]{:S(2)}, u32[]{:S(2)}) %all-to-all-start) | async-done | bytes 524320 | tf_op jit(solution)/shard_map/while/body/eval_jaxpr/all_to_all | solution.py:15
  713.2 29.2 %reduce-scatter.6.cloned.1.call-done = bf16[128,256]{1,0:T(8,128)(2,1)} async-done(((bf16[1024,256]{1,0:T(8,128)(2,1)}), bf16[128,256]{1,0:T(8,128)(2,1)}) %reduce-scatter.6.cloned.1.call-update) | async-done | bytes 65552 | tf_op jit(solution)/shard_map/while
  765.6 17.2 %all-to-all-done = bf16[8,1,256,128]{3,2,1,0:T(8,128)(2,1)S(1)} async-done(((bf16[8,1,256,128]{3,2,1,0:T(8,128)(2,1)}), bf16[8,1,256,128]{3,2,1,0:T(8,128)(2,1)S(1)}, u32[]{:S(2)}, u32[]{:S(2)}) %all-to-all-start) | async-done | bytes 524320 | tf_op jit(solution)/shard_map/while/body/eval_jaxpr/all_to_all | solution.py:15
  785.3 38.9 %reduce-scatter.6.cloned.1.call-done = bf16[128,256]{1,0:T(8,128)(2,1)} async-done(((bf16[1024,256]{1,0:T(8,128)(2,1)}), bf16[128,256]{1,0:T(8,128)(2,1)}) %reduce-scatter.6.cloned.1.call-update) | async-done | bytes 65552 | tf_op jit(solution)/shard_map/while
  839.8 7.7 all-to-all-start
  847.5 17.2 %all-to-all-done = bf16[8,1,256,128]{3,2,1,0:T(8,128)(2,1)S(1)} async-done(((bf16[8,1,256,128]{3,2,1,0:T(8,128)(2,1)}), bf16[8,1,256,128]{3,2,1,0:T(8,128)(2,1)S(1)}, u32[]{:S(2)}, u32[]{:S(2)}) %all-to-all-start) | async-done | bytes 524320 | tf_op jit(solution)/shard_map/while/body/eval_jaxpr/all_to_all | solution.py:15
  867.2 38.9 %reduce-scatter.6.cloned.1.call-done = bf16[128,256]{1,0:T(8,128)(2,1)} async-done(((bf16[1024,256]{1,0:T(8,128)(2,1)}), bf16[128,256]{1,0:T(8,128)(2,1)}) %reduce-scatter.6.cloned.1.call-update) | async-done | bytes 65552 | tf_op jit(solution)/shard_map/while
  931.9 17.2 %all-to-all-done = bf16[8,1,256,128]{3,2,1,0:T(8,128)(2,1)S(1)} async-done(((bf16[8,1,256,128]{3,2,1,0:T(8,128)(2,1)}), bf16[8,1,256,128]{3,2,1,0:T(8,128)(2,1)S(1)}, u32[]{:S(2)}, u32[]{:S(2)}) %all-to-all-start) | async-done | bytes 524320 | tf_op jit(solution)/shard_map/while/body/eval_jaxpr/all_to_all | solution.py:15
  949.1 32.1 %conditional.10 = (f32[9,1024,128]{2,1,0:T(8,128)}) conditional(s32[]{:T(128)} %convert_element_type.705, () %tuple.160, (bf16[1,256,8,128]{3,1,0,2:T(8,128)(2,1)S(1)}, pred[]{:T(512)}, pred[]{:T(512)}, bf16[1,1,256,128]{3,2,1,0:T(8,128)(2,1)}, bf16[1,1,256,128]{3,2,1,0:T(8,128)(2,1)S(1)}, /*index=5*/bf16[1,1,256,128]{3,2,1,0:T(8,128)(2,1)}) %tuple.178), branch_computations={%region_16.16_spmd, %region_17.17_spmd} | conditional | flops 604045312 | bytes 35848256 | solution.py:171
  1006.3 7.7 all-to-all-start
  1014.0 17.2 %all-to-all-done = bf16[8,1,256,128]{3,2,1,0:T(8,128)(2,1)S(1)} async-done(((bf16[8,1,256,128]{3,2,1,0:T(8,128)(2,1)}), bf16[8,1,256,128]{3,2,1,0:T(8,128)(2,1)S(1)}, u32[]{:S(2)}, u32[]{:S(2)}) %all-to-all-start) | async-done | bytes 524320 | tf_op jit(solution)/shard_map/while/body/eval_jaxpr/all_to_all | solution.py:15
  1031.2 32.1 %conditional.10 = (f32[9,1024,128]{2,1,0:T(8,128)}) conditional(s32[]{:T(128)} %convert_element_type.705, () %tuple.160, (bf16[1,256,8,128]{3,1,0,2:T(8,128)(2,1)S(1)}, pred[]{:T(512)}, pred[]{:T(512)}, bf16[1,1,256,128]{3,2,1,0:T(8,128)(2,1)}, bf16[1,1,256,128]{3,2,1,0:T(8,128)(2,1)S(1)}, /*index=5*/bf16[1,1,256,128]{3,2,1,0:T(8,128)(2,1)}) %tuple.178), branch_computations={%region_16.16_spmd, %region_17.17_spmd} | conditional | flops 604045312 | bytes 35848256 | solution.py:171
  1094.6 14.4 %all-to-all-done = bf16[8,1,256,128]{3,2,1,0:T(8,128)(2,1)S(1)} async-done(((bf16[8,1,256,128]{3,2,1,0:T(8,128)(2,1)}), bf16[8,1,256,128]{3,2,1,0:T(8,128)(2,1)S(1)}, u32[]{:S(2)}, u32[]{:S(2)}) %all-to-all-start) | async-done | bytes 524320 | tf_op jit(solution)/shard_map/while/body/eval_jaxpr/all_to_all | solution.py:15
  1109.0 32.1 %conditional.10 = (f32[9,1024,128]{2,1,0:T(8,128)}) conditional(s32[]{:T(128)} %convert_element_type.705, () %tuple.160, (bf16[1,256,8,128]{3,1,0,2:T(8,128)(2,1)S(1)}, pred[]{:T(512)}, pred[]{:T(512)}, bf16[1,1,256,128]{3,2,1,0:T(8,128)(2,1)}, bf16[1,1,256,128]{3,2,1,0:T(8,128)(2,1)S(1)}, /*index=5*/bf16[1,1,256,128]{3,2,1,0:T(8,128)(2,1)}) %tuple.178), branch_computations={%region_16.16_spmd, %region_17.17_spmd} | conditional | flops 604045312 | bytes 35848256 | solution.py:171
  1151.5 17.7 %collective-permute-done.1 = bf16[4,1,256,128]{3,2,1,0:T(8,128)(2,1)S(1)} collective-permute-done((bf16[4,1,256,128]{3,2,1,0:T(8,128)(2,1)}, bf16[4,1,256,128]{3,2,1,0:T(8,128)(2,1)S(1)}, u32[]{:S(2)}, u32[]{:S(2)}) %collective-permute-start.1) | collective-permute-done | bytes 262176 | tf_op jit(solution)/shard_map/while/body/eval_jaxpr/ppermute | solution.py:26
  1181.4 17.4 %all-to-all-done = bf16[8,1,256,128]{3,2,1,0:T(8,128)(2,1)S(1)} async-done(((bf16[8,1,256,128]{3,2,1,0:T(8,128)(2,1)}), bf16[8,1,256,128]{3,2,1,0:T(8,128)(2,1)S(1)}, u32[]{:S(2)}, u32[]{:S(2)}) %all-to-all-start) | async-done | bytes 524320 | tf_op jit(solution)/shard_map/while/body/eval_jaxpr/all_to_all | solution.py:15
  1198.8 32.1 %conditional.10 = (f32[9,1024,128]{2,1,0:T(8,128)}) conditional(s32[]{:T(128)} %convert_element_type.705, () %tuple.160, (bf16[1,256,8,128]{3,1,0,2:T(8,128)(2,1)S(1)}, pred[]{:T(512)}, pred[]{:T(512)}, bf16[1,1,256,128]{3,2,1,0:T(8,128)(2,1)}, bf16[1,1,256,128]{3,2,1,0:T(8,128)(2,1)S(1)}, /*index=5*/bf16[1,1,256,128]{3,2,1,0:T(8,128)(2,1)}) %tuple.178), branch_computations={%region_16.16_spmd, %region_17.17_spmd} | conditional | flops 604045312 | bytes 35848256 | solution.py:171
  1255.4 52.7 %all-reduce.6.cloned.1.call-done = bf16[1,9,1024,128]{3,2,1,0:T(8,128)(2,1)} async-done(((bf16[1,9,1024,128]{3,2,1,0:T(8,128)(2,1)}), bf16[1,9,1024,128]{3,2,1,0:T(8,128)(2,1)}) %all-reduce.6.cloned.1.call-update) | async-done | bytes 2359312 | tf_op jit(solution)/shard_map/psum | solution.py:222
  (1076 shorter events, 563.0 us)
Async XLA Ops:
  31.2 7.1 collective-permute-start
  59.1 9.6 collective-permute-start
  89.9 9.6 collective-permute-start
  120.7 9.6 collective-permute-start
  147.9 19.0 %collective-permute-start = (bf16[4,1,256,128]{3,2,1,0:T(8,128)(2,1)S(1)}, bf16[4,1,256,128]{3,2,1,0:T(8,128)(2,1)S(1)}, u32[]{:S(2)}, u32[]{:S(2)}) collective-permute-start(bf16[4,1,256,128]{3,2,1,0:T(8,128)(2,1)S(1)} %fusion.78), channel_id=1, source_target_pairs={{0,8},{8,16},{16,24},{24,32},{32,40},{40,48},{48,56},{1,9},{9,17},... | collective-permute-start | bytes 786440 | tf_op jit(solution)/shard_map/while/body/eval_jaxpr/ppermute | solution.py:26
  184.4 19.7 %collective-permute-start = (bf16[4,1,256,128]{3,2,1,0:T(8,128)(2,1)S(1)}, bf16[4,1,256,128]{3,2,1,0:T(8,128)(2,1)S(1)}, u32[]{:S(2)}, u32[]{:S(2)}) collective-permute-start(bf16[4,1,256,128]{3,2,1,0:T(8,128)(2,1)S(1)} %fusion.78), channel_id=1, source_target_pairs={{0,8},{8,16},{16,24},{24,32},{32,40},{40,48},{48,56},{1,9},{9,17},... | collective-permute-start | bytes 786440 | tf_op jit(solution)/shard_map/while/body/eval_jaxpr/ppermute | solution.py:26
  221.5 19.6 %collective-permute-start = (bf16[4,1,256,128]{3,2,1,0:T(8,128)(2,1)S(1)}, bf16[4,1,256,128]{3,2,1,0:T(8,128)(2,1)S(1)}, u32[]{:S(2)}, u32[]{:S(2)}) collective-permute-start(bf16[4,1,256,128]{3,2,1,0:T(8,128)(2,1)S(1)} %fusion.78), channel_id=1, source_target_pairs={{0,8},{8,16},{16,24},{24,32},{32,40},{40,48},{48,56},{1,9},{9,17},... | collective-permute-start | bytes 786440 | tf_op jit(solution)/shard_map/while/body/eval_jaxpr/ppermute | solution.py:26
  258.6 19.6 %collective-permute-start = (bf16[4,1,256,128]{3,2,1,0:T(8,128)(2,1)S(1)}, bf16[4,1,256,128]{3,2,1,0:T(8,128)(2,1)S(1)}, u32[]{:S(2)}, u32[]{:S(2)}) collective-permute-start(bf16[4,1,256,128]{3,2,1,0:T(8,128)(2,1)S(1)} %fusion.78), channel_id=1, source_target_pairs={{0,8},{8,16},{16,24},{24,32},{32,40},{40,48},{48,56},{1,9},{9,17},... | collective-permute-start | bytes 786440 | tf_op jit(solution)/shard_map/while/body/eval_jaxpr/ppermute | solution.py:26
  295.7 23.3 %collective-permute-start = (bf16[4,1,256,128]{3,2,1,0:T(8,128)(2,1)S(1)}, bf16[4,1,256,128]{3,2,1,0:T(8,128)(2,1)S(1)}, u32[]{:S(2)}, u32[]{:S(2)}) collective-permute-start(bf16[4,1,256,128]{3,2,1,0:T(8,128)(2,1)S(1)} %fusion.78), channel_id=1, source_target_pairs={{0,8},{8,16},{16,24},{24,32},{32,40},{40,48},{48,56},{1,9},{9,17},... | collective-permute-start | bytes 786440 | tf_op jit(solution)/shard_map/while/body/eval_jaxpr/ppermute | solution.py:26
  336.5 19.6 %collective-permute-start = (bf16[4,1,256,128]{3,2,1,0:T(8,128)(2,1)S(1)}, bf16[4,1,256,128]{3,2,1,0:T(8,128)(2,1)S(1)}, u32[]{:S(2)}, u32[]{:S(2)}) collective-permute-start(bf16[4,1,256,128]{3,2,1,0:T(8,128)(2,1)S(1)} %fusion.78), channel_id=1, source_target_pairs={{0,8},{8,16},{16,24},{24,32},{32,40},{40,48},{48,56},{1,9},{9,17},... | collective-permute-start | bytes 786440 | tf_op jit(solution)/shard_map/while/body/eval_jaxpr/ppermute | solution.py:26
  373.6 23.3 %collective-permute-start = (bf16[4,1,256,128]{3,2,1,0:T(8,128)(2,1)S(1)}, bf16[4,1,256,128]{3,2,1,0:T(8,128)(2,1)S(1)}, u32[]{:S(2)}, u32[]{:S(2)}) collective-permute-start(bf16[4,1,256,128]{3,2,1,0:T(8,128)(2,1)S(1)} %fusion.78), channel_id=1, source_target_pairs={{0,8},{8,16},{16,24},{24,32},{32,40},{40,48},{48,56},{1,9},{9,17},... | collective-permute-start | bytes 786440 | tf_op jit(solution)/shard_map/while/body/eval_jaxpr/ppermute | solution.py:26
  397.0 72.9 %reduce-scatter.6.cloned.1.call-start = ((), (), s32[]{:S(2)}) async-start(), calls=%async_computation.3 | async-start | bytes 589824 | tf_op jit(solution)/shard_map/while
  401.7 18.8 %all-to-all-start = ((bf16[8,1,256,128]{3,2,1,0:T(8,128)(2,1)}), bf16[8,1,256,128]{3,2,1,0:T(8,128)(2,1)S(1)}, u32[]{:S(2)}, u32[]{:S(2)}) async-start(bf16[8,1,256,128]{3,2,1,0:T(8,128)(2,1)} %stack.29), calls=%async_computation.1 | async-start | bytes 1048576 | tf_op jit(solution)/shard_map/while/body/eval_jaxpr/all_to_all | solution.py:15
  472.5 7.3 collective-permute-start.1
  479.9 48.1 %reduce-scatter.6.cloned.1.call-start = ((), (), s32[]{:S(2)}) async-start(), calls=%async_computation.3 | async-start | bytes 589824 | tf_op jit(solution)/shard_map/while
  484.6 22.9 %all-to-all-start = ((bf16[8,1,256,128]{3,2,1,0:T(8,128)(2,1)}), bf16[8,1,256,128]{3,2,1,0:T(8,128)(2,1)S(1)}, u32[]{:S(2)}, u32[]{:S(2)}) async-start(bf16[8,1,256,128]{3,2,1,0:T(8,128)(2,1)} %stack.29), calls=%async_computation.1 | async-start | bytes 1048576 | tf_op jit(solution)/shard_map/while/body/eval_jaxpr/all_to_all | solution.py:15
  530.5 7.8 collective-permute-start.1
  538.9 56.2 %reduce-scatter.6.cloned.1.call-start = ((), (), s32[]{:S(2)}) async-start(), calls=%async_computation.3 | async-start | bytes 589824 | tf_op jit(solution)/shard_map/while
  543.6 22.1 %all-to-all-start = ((bf16[8,1,256,128]{3,2,1,0:T(8,128)(2,1)}), bf16[8,1,256,128]{3,2,1,0:T(8,128)(2,1)S(1)}, u32[]{:S(2)}, u32[]{:S(2)}) async-start(bf16[8,1,256,128]{3,2,1,0:T(8,128)(2,1)} %stack.29), calls=%async_computation.1 | async-start | bytes 1048576 | tf_op jit(solution)/shard_map/while/body/eval_jaxpr/all_to_all | solution.py:15
  597.7 7.8 collective-permute-start.1
  606.0 61.8 %reduce-scatter.6.cloned.1.call-start = ((), (), s32[]{:S(2)}) async-start(), calls=%async_computation.3 | async-start | bytes 589824 | tf_op jit(solution)/shard_map/while
  610.7 22.0 %all-to-all-start = ((bf16[8,1,256,128]{3,2,1,0:T(8,128)(2,1)}), bf16[8,1,256,128]{3,2,1,0:T(8,128)(2,1)S(1)}, u32[]{:S(2)}, u32[]{:S(2)}) async-start(bf16[8,1,256,128]{3,2,1,0:T(8,128)(2,1)} %stack.29), calls=%async_computation.1 | async-start | bytes 1048576 | tf_op jit(solution)/shard_map/while/body/eval_jaxpr/all_to_all | solution.py:15
  670.4 7.8 collective-permute-start.1
  678.7 63.8 %reduce-scatter.6.cloned.1.call-start = ((), (), s32[]{:S(2)}) async-start(), calls=%async_computation.3 | async-start | bytes 589824 | tf_op jit(solution)/shard_map/while
  683.4 27.3 %all-to-all-start = ((bf16[8,1,256,128]{3,2,1,0:T(8,128)(2,1)}), bf16[8,1,256,128]{3,2,1,0:T(8,128)(2,1)S(1)}, u32[]{:S(2)}, u32[]{:S(2)}) async-start(bf16[8,1,256,128]{3,2,1,0:T(8,128)(2,1)} %stack.29), calls=%async_computation.1 | async-start | bytes 1048576 | tf_op jit(solution)/shard_map/while/body/eval_jaxpr/all_to_all | solution.py:15
  745.0 7.8 collective-permute-start.1
  753.4 70.8 %reduce-scatter.6.cloned.1.call-start = ((), (), s32[]{:S(2)}) async-start(), calls=%async_computation.3 | async-start | bytes 589824 | tf_op jit(solution)/shard_map/while
  758.1 24.6 %all-to-all-start = ((bf16[8,1,256,128]{3,2,1,0:T(8,128)(2,1)}), bf16[8,1,256,128]{3,2,1,0:T(8,128)(2,1)S(1)}, u32[]{:S(2)}, u32[]{:S(2)}) async-start(bf16[8,1,256,128]{3,2,1,0:T(8,128)(2,1)} %stack.29), calls=%async_computation.1 | async-start | bytes 1048576 | tf_op jit(solution)/shard_map/while/body/eval_jaxpr/all_to_all | solution.py:15
  826.8 7.8 collective-permute-start.1
  835.1 71.0 %reduce-scatter.6.cloned.1.call-start = ((), (), s32[]{:S(2)}) async-start(), calls=%async_computation.3 | async-start | bytes 589824 | tf_op jit(solution)/shard_map/while
  839.8 24.9 %all-to-all-start = ((bf16[8,1,256,128]{3,2,1,0:T(8,128)(2,1)}), bf16[8,1,256,128]{3,2,1,0:T(8,128)(2,1)S(1)}, u32[]{:S(2)}, u32[]{:S(2)}) async-start(bf16[8,1,256,128]{3,2,1,0:T(8,128)(2,1)} %stack.29), calls=%async_computation.1 | async-start | bytes 1048576 | tf_op jit(solution)/shard_map/while/body/eval_jaxpr/all_to_all | solution.py:15
  908.7 7.8 collective-permute-start.1
  917.1 70.9 %reduce-scatter.6.cloned.1.call-start = ((), (), s32[]{:S(2)}) async-start(), calls=%async_computation.3 | async-start | bytes 589824 | tf_op jit(solution)/shard_map/while
  924.5 24.6 %all-to-all-start = ((bf16[8,1,256,128]{3,2,1,0:T(8,128)(2,1)}), bf16[8,1,256,128]{3,2,1,0:T(8,128)(2,1)S(1)}, u32[]{:S(2)}, u32[]{:S(2)}) async-start(bf16[8,1,256,128]{3,2,1,0:T(8,128)(2,1)} %stack.29), calls=%async_computation.1 | async-start | bytes 1048576 | tf_op jit(solution)/shard_map/while/body/eval_jaxpr/all_to_all | solution.py:15
  990.5 7.8 collective-permute-start.1
  998.9 68.2 %reduce-scatter.6.cloned.1.call-start = ((), (), s32[]{:S(2)}) async-start(), calls=%async_computation.3 | async-start | bytes 589824 | tf_op jit(solution)/shard_map/while
  1006.3 24.9 %all-to-all-start = ((bf16[8,1,256,128]{3,2,1,0:T(8,128)(2,1)}), bf16[8,1,256,128]{3,2,1,0:T(8,128)(2,1)S(1)}, u32[]{:S(2)}, u32[]{:S(2)}) async-start(bf16[8,1,256,128]{3,2,1,0:T(8,128)(2,1)} %stack.29), calls=%async_computation.1 | async-start | bytes 1048576 | tf_op jit(solution)/shard_map/while/body/eval_jaxpr/all_to_all | solution.py:15
  1069.7 12.5 collective-permute-start.1
  1082.2 58.8 %reduce-scatter.6.cloned.1.call-start = ((), (), s32[]{:S(2)}) async-start(), calls=%async_computation.3 | async-start | bytes 589824 | tf_op jit(solution)/shard_map/while
  1089.7 19.3 %all-to-all-start = ((bf16[8,1,256,128]{3,2,1,0:T(8,128)(2,1)}), bf16[8,1,256,128]{3,2,1,0:T(8,128)(2,1)S(1)}, u32[]{:S(2)}, u32[]{:S(2)}) async-start(bf16[8,1,256,128]{3,2,1,0:T(8,128)(2,1)} %stack.29), calls=%async_computation.1 | async-start | bytes 1048576 | tf_op jit(solution)/shard_map/while/body/eval_jaxpr/all_to_all | solution.py:15
  1143.7 25.5 %collective-permute-start.1 = (bf16[4,1,256,128]{3,2,1,0:T(8,128)(2,1)}, bf16[4,1,256,128]{3,2,1,0:T(8,128)(2,1)S(1)}, u32[]{:S(2)}, u32[]{:S(2)}) collective-permute-start(bf16[4,1,256,128]{3,2,1,0:T(8,128)(2,1)} %fusion.82), channel_id=1, source_target_pairs={{8,0},{16,8},{24,16},{32,24},{40,32},{48,40},{56,48},{9,1},{17,9},... | collective-permute-start | bytes 786440 | tf_op jit(solution)/shard_map/while/body/eval_jaxpr/ppermute | solution.py:26
  1145.0 24.2 %copy-start.13 = (f32[4,1,4]{2,1,0:T(1,128)S(1)}, f32[4,1,4]{2,1,0:T(1,128)}, u32[]{:S(2)}) copy-start(f32[4,1,4]{2,1,0:T(1,128)} %copy-done.12) | copy-start | bytes 196 | tf_op jit(solution)/shard_map/while
  1145.0 24.2 %copy-start.15 = (f32[4,1,4]{2,1,0:T(1,128)S(1)}, f32[4,1,4]{2,1,0:T(1,128)}, u32[]{:S(2)}) copy-start(f32[4,1,4]{2,1,0:T(1,128)} %copy-done.14) | copy-start | bytes 196 | tf_op jit(solution)/shard_map/while
  1151.5 17.7 %copy-start.7 = (f32[128]{0:T(128)}, f32[128]{0:T(128)S(1)}, u32[]{:S(2)}) copy-start(f32[128]{0:T(128)S(1)} %get-tuple-element.1596) | copy-start | bytes 1540 | tf_op jit(solution)/shard_map/while
  1169.3 61.6 %reduce-scatter.6.cloned.1.call-start = ((), (), s32[]{:S(2)}) async-start(), calls=%async_computation.3 | async-start | bytes 589824 | tf_op jit(solution)/shard_map/while
  1176.7 22.1 %all-to-all-start = ((bf16[8,1,256,128]{3,2,1,0:T(8,128)(2,1)}), bf16[8,1,256,128]{3,2,1,0:T(8,128)(2,1)S(1)}, u32[]{:S(2)}, u32[]{:S(2)}) async-start(bf16[8,1,256,128]{3,2,1,0:T(8,128)(2,1)} %stack.29), calls=%async_computation.1 | async-start | bytes 1048576 | tf_op jit(solution)/shard_map/while/body/eval_jaxpr/all_to_all | solution.py:15
  1233.5 9.1 collective-permute-start.1
  1242.6 65.5 %all-reduce.6.cloned.1.call-start = ((), (), s32[]{:S(2)}) async-start(), calls=%async_computation.2 | async-start | bytes 4718592 | tf_op jit(solution)/shard_map/psum | solution.py:222
  (132 other events, 574.3 us)
Sparse Core Ops, SparseCore 0:
  400.6 69.2 reduce-scatter.5
  483.4 44.4 reduce-scatter.5
  542.4 52.5 reduce-scatter.5
  609.5 58.1 reduce-scatter.5
  682.2 60.1 reduce-scatter.5
  756.9 67.2 reduce-scatter.5
  838.7 67.4 reduce-scatter.5
  923.3 64.5 reduce-scatter.5
  1005.2 61.8 reduce-scatter.5
  1088.5 41.5 reduce-scatter.5
  1175.5 27.1 reduce-scatter.5
Sparse Core Ops, SparseCore 1:
  1247.0 61.1 all-reduce.5
